TPU v7x, 32 devices: a whole 2x2x4 slice. The times are simulated.
32 devices in a mesh: tile: 8 (over z, x), wave: 4 (over y, core).
Axes of the slice: x: 2, y: 2, z: 4, core: 2. Of those that a mesh axis runs over, the one named last changes fastest.
Arguments:
- fibre_data: bfloat16 [128, 256, 128], P('wave', 'tile'), may hold values from -162 to 162
- kernels: bfloat16 [4, 256, 4, 128, 128], P('wave', 'tile'), may hold values from -0.25 to 0.25
- block_index: int32 [4, 256, 4], P('wave', 'tile'), may hold values from 0 to 127, as said below
- live_count: int32 [8], P('tile'), may hold values from 8 to 32, as said below
Outputs:
- solution: float32 [128, 128, 128], P('wave', 'tile')
- residual: float32 [128, 128, 128], P('wave', 'tile')
Inputs may be any that keep to these rules, and one draw needn't show every extreme that they name: `block_index`: A group of tile t (groups t * 32 to (t + 1) * 32 - 1) names only blocks from max(t * 16 - 4, 0) to min((t + 1) * 16 + 4, 128) - 1; for every kernel set and tile, some live group of that tile names both ends of that range. `live_count`: some tile has all 32 groups live.
All inputs are finite; a program needn't handle non-finite values.
Results may differ from a plain program's by a relative error of at most 0.035.
Values may be sent and summed in bfloat16 or wider, within the bound.
No kernel may reach another device: no remote copies, remote signals or barrier semaphores. Data moves between devices by JAX's collectives and lax.ppermute only.
A program may use at most 64 MiB of HBM per device.

v0:
```python
import jax
import jax.numpy as jnp
from jax import lax
from jax.sharding import PartitionSpec as P

HALO_BLOCKS = 4
BLOCKS_DEV = 16
ITERATIONS = 3
TIKHONOV = 0.5


def from_behind(value, axis, by):
    size = lax.axis_size(axis)
    pairs = [(i, i + by) for i in range(size) if 0 <= i + by < size]
    return lax.ppermute(value, axis, pairs)


def extended(value, sides, width):
    for axis, dim in sides:
        size, length = (lax.axis_size(axis), value.shape[dim])
        up = [(i, (i + 1) % size) for i in range(size - 1)]
        down = [(j, i) for i, j in up]
        last = lax.slice_in_dim(value, length - width, length, axis=dim)
        initial = lax.slice_in_dim(value, 0, width, axis=dim)
        before = lax.ppermute(last, axis, up)
        after = lax.ppermute(initial, axis, down)
        value = jnp.concatenate([before, value, after], axis=dim)
    return value


def select_table(local_index, extent):
    return (local_index[..., None] == jnp.arange(extent, dtype=jnp.int32)).astype(jnp.bfloat16)


def forward_image(window16, kernels, selector16, live_mask):
    kernel_sets = kernels.shape[0]
    shaped = window16.reshape(
        kernel_sets, window16.shape[0] // kernel_sets, window16.shape[1], window16.shape[2]
    )
    picked = jnp.einsum(
        "cgrb,cwbs->cwgrs", selector16, shaped, preferred_element_type=jnp.float32
    ).astype(jnp.bfloat16)
    applied = jnp.einsum("cwgrs,cgrsf->cwgf", picked, kernels, preferred_element_type=jnp.float32)
    return (applied * live_mask[None, None, :, None]).astype(jnp.bfloat16)


def adjoint_image(image16, kernels, selector16):
    spread = jnp.einsum("cwgf,cgrsf->cwgrs", image16, kernels, preferred_element_type=jnp.float32)
    upper_part = spread.astype(jnp.bfloat16)
    lower_part = (spread - upper_part.astype(jnp.float32)).astype(jnp.bfloat16)
    summed = jnp.einsum(
        "cgrb,cwgrs->cwbs", selector16, upper_part, preferred_element_type=jnp.float32
    )
    summed = summed + jnp.einsum(
        "cgrb,cwgrs->cwbs", selector16, lower_part, preferred_element_type=jnp.float32
    )
    return summed.reshape(summed.shape[0] * summed.shape[1], summed.shape[2], summed.shape[3])


def shards(fibre_data, kernels, block_index, live_count):
    extent = BLOCKS_DEV + 2 * HALO_BLOCKS
    first_block = lax.axis_index("tile") * BLOCKS_DEV - HALO_BLOCKS
    selector16 = select_table(block_index - first_block, extent)
    groups = block_index.shape[1]
    live_mask = (jnp.arange(groups, dtype=jnp.int32) < live_count[0]).astype(jnp.float32)
    kernel_sets = kernels.shape[0]
    observed = fibre_data * live_mask.astype(jnp.bfloat16)[None, :, None]
    observed = observed.reshape(
        kernel_sets, fibre_data.shape[0] // kernel_sets, groups, fibre_data.shape[2]
    )
    partial_rhs = adjoint_image(observed, kernels, selector16)
    rim_width = HALO_BLOCKS

    def settle(partial_value):
        owned_part = partial_value[:, rim_width : rim_width + BLOCKS_DEV]
        from_right = from_behind(
            partial_value[:, :rim_width].astype(jnp.bfloat16), "tile", -1
        ).astype(jnp.float32)
        from_left = from_behind(
            partial_value[:, BLOCKS_DEV + rim_width :].astype(jnp.bfloat16), "tile", 1
        ).astype(jnp.float32)
        owned_part = owned_part.at[:, :rim_width].add(from_left)
        return owned_part.at[:, BLOCKS_DEV - rim_width :].add(from_right)

    def operate(vector):
        padded = extended(vector.astype(jnp.bfloat16), (("tile", 1),), HALO_BLOCKS)
        image16 = forward_image(padded, kernels, selector16, live_mask)
        return settle(adjoint_image(image16, kernels, selector16)) + TIKHONOV * vector

    def local_inner(first_vector, second_vector):
        return jnp.sum(first_vector * second_vector)

    rhs = settle(partial_rhs)
    solution = jnp.zeros_like(rhs)
    residual = rhs

    def paired(vector, applied):
        return lax.psum(
            (local_inner(vector, vector), local_inner(vector, applied)), ("tile", "wave")
        )

    applied = operate(residual)
    current, product = paired(residual, applied)
    step_size = current / product
    direction = residual
    applied_dir = applied
    for iteration in range(ITERATIONS):
        solution = solution + step_size * direction
        residual = residual - step_size * applied_dir
        if iteration + 1 < ITERATIONS:
            applied = operate(residual)
            following, product = paired(residual, applied)
            beta_ratio = following / current
            step_size = following / (product - beta_ratio * following / step_size)
            direction = residual + beta_ratio * direction
            applied_dir = applied + beta_ratio * applied_dir
            current = following
    return (solution, residual)


def solution(mesh):
    in_specs = (
        P("wave", "tile", None),
        P("wave", "tile", None, None, None),
        P("wave", "tile", None),
        P("tile"),
    )
    out_specs = (P("wave", "tile", None), P("wave", "tile", None))
    return jax.shard_map(shards, mesh=mesh, in_specs=in_specs, out_specs=out_specs, check_vma=False)
```

profile of v0, /device:TPU:0, one launch (start us, length us, event | category | flops | bytes accessed | tf_op | source)
XLA Modules:
  0.0 242.5 jit_solution(4463199943497567733)
XLA Ops:
  1.3 1.0 multiply_bitcast_fusion
  2.3 3.7 %fusion.12 = f32[32,32,4,128]{3,1,2,0:T(8,128)S(1)} fusion(bf16[1,32,4,128,128]{4,3,2,1,0:T(8,128)(2,1)} %param.21, bf16[32,32,128,1]{2,1,0,3:T(8,128)(2,1)S(1)} %multiply_bitcast_fusion), kind=kOutput, calls=%fused_computation.12 | convolution fusion | flops 134217728 | bytes 6553600 | tf_op jit(solution)/shard_map/cwgf,cgrsf->cwgrs/dot_general | solution.py:48
  6.1 0.3 fusion.71
  6.4 0.0 copy-start.4
  6.4 0.3 fusion.89
  6.6 0.4 copy-done.4
  7.0 0.7 convolution_bitcast_fusion.6
  7.7 0.7 fusion.153
  8.4 4.9 %collective-permute-start = (bf16[32,4,128]{2,1,0:T(4,128)(2,1)S(1)}, bf16[32,4,128]{2,1,0:T(4,128)(2,1)S(1)}, u32[]{:S(2)}, u32[]{:S(2)}) collective-permute-start(bf16[32,4,128]{2,1,0:T(4,128)(2,1)S(1)} %get-tuple-element.124), channel_id=1, source_target_pairs={{0,4},{4,8},{8,12},{12,16},{16,20},{20,24},{24,28},{1,5},{5,9},{9,... | collective-permute-start | bytes 98312 | tf_op jit(solution)/shard_map/ppermute | solution.py:15
  13.3 1.3 collective-permute-start.1
  14.7 0.2 collective-permute-done
  14.9 4.2 %collective-permute-done.1 = bf16[32,4,128]{2,1,0:T(4,128)(2,1)S(1)} collective-permute-done((bf16[32,4,128]{2,1,0:T(4,128)(2,1)S(1)}, bf16[32,4,128]{2,1,0:T(4,128)(2,1)S(1)}, u32[]{:S(2)}, u32[]{:S(2)}) %collective-permute-start.1) | collective-permute-done | bytes 32800 | tf_op jit(solution)/shard_map/ppermute | solution.py:15
  19.2 1.3 collective-permute-start.3
  20.5 5.0 %collective-permute-start.2 = (bf16[32,4,128]{2,1,0:T(4,128)(2,1)S(1)}, bf16[32,4,128]{2,1,0:T(4,128)(2,1)S(1)}, u32[]{:S(2)}, u32[]{:S(2)}) collective-permute-start(bf16[32,4,128]{2,1,0:T(4,128)(2,1)S(1)} %get-tuple-element.129), channel_id=1, source_target_pairs={{0,4},{4,8},{8,12},{12,16},{16,20},{20,24},{24,28},{1,5},{5,9},{9,... | collective-permute-start | bytes 98312 | tf_op jit(solution)/shard_map/ppermute | solution.py:25
  25.5 0.0 collective-permute-done.3
  25.6 1.6 collective-permute-done.2
  27.1 0.5 fusion.18
  27.6 6.0 %fusion.8 = f32[32,32,4,128]{3,1,2,0:T(8,128)S(1)} fusion(bf16[1,32,4,128,128]{4,3,2,1,0:T(8,128)(2,1)} %param.21, bf16[32,32,4,128]{3,1,2,0:T(8,128)(2,1)S(1)} %fusion.18, f32[32]{0:T(128)S(1)} %compare_convert_fusion), kind=kOutput, calls=%fused_computation.8 | convolution fusion | flops 268697600 | bytes 7340160 | tf_op jit(solution)/shard_map/cwgf,cgrsf->cwgrs/dot_general | solution.py:48
  33.6 0.3 fusion.72
  33.9 0.2 fusion.90
  34.2 0.7 convolution_bitcast_fusion.4
  34.8 0.7 fusion.154
  35.6 4.8 %collective-permute-start.4 = (bf16[32,4,128]{2,1,0:T(4,128)(2,1)S(1)}, bf16[32,4,128]{2,1,0:T(4,128)(2,1)S(1)}, u32[]{:S(2)}, u32[]{:S(2)}) collective-permute-start(bf16[32,4,128]{2,1,0:T(4,128)(2,1)S(1)} %get-tuple-element.122), channel_id=1, source_target_pairs={{0,4},{4,8},{8,12},{12,16},{16,20},{20,24},{24,28},{1,5},{5,9},{9,... | collective-permute-start | bytes 98312 | tf_op jit(solution)/shard_map/ppermute | solution.py:15
  40.4 1.3 collective-permute-start.5
  41.7 0.2 collective-permute-done.4
  42.0 5.4 %collective-permute-done.5 = bf16[32,4,128]{2,1,0:T(4,128)(2,1)S(1)} collective-permute-done((bf16[32,4,128]{2,1,0:T(4,128)(2,1)S(1)}, bf16[32,4,128]{2,1,0:T(4,128)(2,1)S(1)}, u32[]{:S(2)}, u32[]{:S(2)}) %collective-permute-start.5) | collective-permute-done | bytes 32800 | tf_op jit(solution)/shard_map/ppermute | solution.py:15
  47.5 0.7 multiply_reduce_fusion.4
  48.2 42.1 %all-reduce.2 = (f32[]{:T(128)}, f32[]{:T(128)}) all-reduce(f32[]{:T(128)} %get-tuple-element.103, f32[]{:T(128)} %get-tuple-element.102), channel_id=1, replica_groups=mesh['tile'=8,'wave'=4] {'tile','wave'}, use_global_device_ids=true, to_apply=%region_1.0 | all-reduce | flops 2 | bytes 16 | tf_op jit(solution)/shard_map/psum | solution.py:98
  91.7 0.0 copy-start
  91.7 1.3 collective-permute-start.7
  93.0 5.0 %collective-permute-start.6 = (bf16[32,4,128]{2,1,0:T(4,128)(2,1)S(1)}, bf16[32,4,128]{2,1,0:T(4,128)(2,1)S(1)}, u32[]{:S(2)}, u32[]{:S(2)}) collective-permute-start(bf16[32,4,128]{2,1,0:T(4,128)(2,1)S(1)} %get-tuple-element.127), channel_id=1, source_target_pairs={{0,4},{4,8},{8,12},{12,16},{16,20},{20,24},{24,28},{1,5},{5,9},{9,... | collective-permute-start | bytes 98312 | tf_op jit(solution)/shard_map/ppermute | solution.py:25
  98.0 0.0 collective-permute-done.7
  98.0 1.4 collective-permute-done.6
  99.4 1.5 fusion.19
  100.8 6.3 %fusion.4 = f32[32,32,4,128]{3,1,2,0:T(8,128)S(1)} fusion(bf16[1,32,4,128,128]{4,3,2,1,0:T(8,128)(2,1)} %param.21, bf16[32,32,4,128]{3,1,2,0:T(8,128)(2,1)} %fusion.19, f32[32]{0:T(128)S(1)} %compare_convert_fusion), kind=kOutput, calls=%fused_computation.4 | convolution fusion | flops 268697600 | bytes 7340160 | tf_op jit(solution)/shard_map/cwgf,cgrsf->cwgrs/dot_general | solution.py:48
  107.2 0.3 fusion.73
  107.4 0.2 fusion.91
  107.7 0.7 convolution_bitcast_fusion.2
  108.4 0.7 fusion.155
  109.1 4.8 %collective-permute-start.8 = (bf16[32,4,128]{2,1,0:T(4,128)(2,1)S(1)}, bf16[32,4,128]{2,1,0:T(4,128)(2,1)S(1)}, u32[]{:S(2)}, u32[]{:S(2)}) collective-permute-start(bf16[32,4,128]{2,1,0:T(4,128)(2,1)S(1)} %get-tuple-element.120), channel_id=1, source_target_pairs={{0,4},{4,8},{8,12},{12,16},{16,20},{20,24},{24,28},{1,5},{5,9},{9,... | collective-permute-start | bytes 98312 | tf_op jit(solution)/shard_map/ppermute | solution.py:15
  113.9 1.3 collective-permute-start.9
  115.2 0.2 collective-permute-done.8
  115.5 5.4 %collective-permute-done.9 = bf16[32,4,128]{2,1,0:T(4,128)(2,1)S(1)} collective-permute-done((bf16[32,4,128]{2,1,0:T(4,128)(2,1)S(1)}, bf16[32,4,128]{2,1,0:T(4,128)(2,1)S(1)}, u32[]{:S(2)}, u32[]{:S(2)}) %collective-permute-start.9) | collective-permute-done | bytes 32800 | tf_op jit(solution)/shard_map/ppermute | solution.py:15
  121.0 0.7 multiply_reduce_fusion.2
  121.7 39.7 %all-reduce.1 = (f32[]{:T(128)}, f32[]{:T(128)}) all-reduce(f32[]{:T(128)} %get-tuple-element.101, f32[]{:T(128)} %get-tuple-element.100), channel_id=1, replica_groups=mesh['tile'=8,'wave'=4] {'tile','wave'}, use_global_device_ids=true, to_apply=%region_5.0 | all-reduce | flops 2 | bytes 16 | tf_op jit(solution)/shard_map/psum | solution.py:98
  166.0 0.9 fusion.144
  166.9 1.3 collective-permute-start.11
  168.2 4.8 %collective-permute-start.10 = (bf16[32,4,128]{2,1,0:T(4,128)(2,1)S(1)}, bf16[32,4,128]{2,1,0:T(4,128)(2,1)S(1)}, u32[]{:S(2)}, u32[]{:S(2)}) collective-permute-start(bf16[32,4,128]{2,1,0:T(4,128)(2,1)S(1)} %get-tuple-element.125), channel_id=1, source_target_pairs={{0,4},{4,8},{8,12},{12,16},{16,20},{20,24},{24,28},{1,5},{5,9},{9,... | collective-permute-start | bytes 98312 | tf_op jit(solution)/shard_map/ppermute | solution.py:25
  173.0 0.0 collective-permute-done.11
  173.0 1.6 collective-permute-done.10
  174.6 0.5 fusion.20
  175.1 6.0 %fusion = f32[32,32,4,128]{3,1,2,0:T(8,128)S(1)} fusion(bf16[1,32,4,128,128]{4,3,2,1,0:T(8,128)(2,1)} %param.21, bf16[32,32,4,128]{3,1,2,0:T(8,128)(2,1)S(1)} %fusion.20, f32[32]{0:T(128)S(1)} %compare_convert_fusion), kind=kOutput, calls=%fused_computation | convolution fusion | flops 268697600 | bytes 7340160 | tf_op jit(solution)/shard_map/cwgf,cgrsf->cwgrs/dot_general | solution.py:48
  181.1 0.3 fusion.74
  181.4 0.2 fusion.92
  181.7 0.0 copy-start.2
  181.7 0.7 convolution_bitcast_fusion
  182.4 0.7 fusion.156
  183.1 4.8 %collective-permute-start.12 = (bf16[32,4,128]{2,1,0:T(4,128)(2,1)S(1)}, bf16[32,4,128]{2,1,0:T(4,128)(2,1)S(1)}, u32[]{:S(2)}, u32[]{:S(2)}) collective-permute-start(bf16[32,4,128]{2,1,0:T(4,128)(2,1)S(1)} %get-tuple-element.118), channel_id=1, source_target_pairs={{0,4},{4,8},{8,12},{12,16},{16,20},{20,24},{24,28},{1,5},{5,9},{9,... | collective-permute-start | bytes 98312 | tf_op jit(solution)/shard_map/ppermute | solution.py:15
  187.9 1.3 collective-permute-start.13
  189.2 0.2 collective-permute-done.12
  189.5 5.4 %collective-permute-done.13 = bf16[32,4,128]{2,1,0:T(4,128)(2,1)S(1)} collective-permute-done((bf16[32,4,128]{2,1,0:T(4,128)(2,1)S(1)}, bf16[32,4,128]{2,1,0:T(4,128)(2,1)S(1)}, u32[]{:S(2)}, u32[]{:S(2)}) %collective-permute-start.13) | collective-permute-done | bytes 32800 | tf_op jit(solution)/shard_map/ppermute | solution.py:15
  195.0 0.7 multiply_reduce_fusion
  195.7 42.1 %all-reduce = (f32[]{:T(128)}, f32[]{:T(128)}) all-reduce(f32[]{:T(128)} %get-tuple-element.99, f32[]{:T(128)} %get-tuple-element.98), channel_id=1, replica_groups=mesh['tile'=8,'wave'=4] {'tile','wave'}, use_global_device_ids=true, to_apply=%region_9.0 | all-reduce | flops 2 | bytes 16 | tf_op jit(solution)/shard_map/psum | solution.py:98
  241.6 0.9 multiply_subtract_fusion
  (30 shorter events, 0.7 us)
Async XLA Ops:
  6.4 0.7 copy-start.4
  8.4 6.5 %collective-permute-start = (bf16[32,4,128]{2,1,0:T(4,128)(2,1)S(1)}, bf16[32,4,128]{2,1,0:T(4,128)(2,1)S(1)}, u32[]{:S(2)}, u32[]{:S(2)}) collective-permute-start(bf16[32,4,128]{2,1,0:T(4,128)(2,1)S(1)} %get-tuple-element.124), channel_id=1, source_target_pairs={{0,4},{4,8},{8,12},{12,16},{16,20},{20,24},{24,28},{1,5},{5,9},{9,... | collective-permute-start | bytes 98312 | tf_op jit(solution)/shard_map/ppermute | solution.py:15
  13.3 5.8 %collective-permute-start.1 = (bf16[32,4,128]{2,1,0:T(4,128)(2,1)S(1)}, bf16[32,4,128]{2,1,0:T(4,128)(2,1)S(1)}, u32[]{:S(2)}, u32[]{:S(2)}) collective-permute-start(bf16[32,4,128]{2,1,0:T(4,128)(2,1)S(1)} %get-tuple-element.123), channel_id=1, source_target_pairs={{4,0},{8,4},{12,8},{16,12},{20,16},{24,20},{28,24},{5,1},{9,5},{13... | collective-permute-start | bytes 98312 | tf_op jit(solution)/shard_map/ppermute | solution.py:15
  19.2 6.3 %collective-permute-start.3 = (bf16[32,4,128]{2,1,0:T(4,128)(2,1)S(1)}, bf16[32,4,128]{2,1,0:T(4,128)(2,1)S(1)}, u32[]{:S(2)}, u32[]{:S(2)}) collective-permute-start(bf16[32,4,128]{2,1,0:T(4,128)(2,1)S(1)} %get-tuple-element.130), channel_id=1, source_target_pairs={{4,0},{8,4},{12,8},{16,12},{20,16},{24,20},{28,24},{5,1},{9,5},{13... | collective-permute-start | bytes 98312 | tf_op jit(solution)/shard_map/ppermute | solution.py:26
  20.5 6.6 %collective-permute-start.2 = (bf16[32,4,128]{2,1,0:T(4,128)(2,1)S(1)}, bf16[32,4,128]{2,1,0:T(4,128)(2,1)S(1)}, u32[]{:S(2)}, u32[]{:S(2)}) collective-permute-start(bf16[32,4,128]{2,1,0:T(4,128)(2,1)S(1)} %get-tuple-element.129), channel_id=1, source_target_pairs={{0,4},{4,8},{8,12},{12,16},{16,20},{20,24},{24,28},{1,5},{5,9},{9,... | collective-permute-start | bytes 98312 | tf_op jit(solution)/shard_map/ppermute | solution.py:25
  35.6 6.4 %collective-permute-start.4 = (bf16[32,4,128]{2,1,0:T(4,128)(2,1)S(1)}, bf16[32,4,128]{2,1,0:T(4,128)(2,1)S(1)}, u32[]{:S(2)}, u32[]{:S(2)}) collective-permute-start(bf16[32,4,128]{2,1,0:T(4,128)(2,1)S(1)} %get-tuple-element.122), channel_id=1, source_target_pairs={{0,4},{4,8},{8,12},{12,16},{16,20},{20,24},{24,28},{1,5},{5,9},{9,... | collective-permute-start | bytes 98312 | tf_op jit(solution)/shard_map/ppermute | solution.py:15
  40.4 7.0 %collective-permute-start.5 = (bf16[32,4,128]{2,1,0:T(4,128)(2,1)S(1)}, bf16[32,4,128]{2,1,0:T(4,128)(2,1)S(1)}, u32[]{:S(2)}, u32[]{:S(2)}) collective-permute-start(bf16[32,4,128]{2,1,0:T(4,128)(2,1)S(1)} %get-tuple-element.121), channel_id=1, source_target_pairs={{4,0},{8,4},{12,8},{16,12},{20,16},{24,20},{28,24},{5,1},{9,5},{13... | collective-permute-start | bytes 98312 | tf_op jit(solution)/shard_map/ppermute | solution.py:15
  91.7 74.3 %copy-start = (f32[32,16,128]{2,1,0:T(8,128)}, f32[32,16,128]{2,1,0:T(8,128)S(1)}, u32[]{:S(2)}) copy-start(f32[32,16,128]{2,1,0:T(8,128)S(1)} %get-tuple-element.114) | copy-start | bytes 786436
  91.7 6.3 %collective-permute-start.7 = (bf16[32,4,128]{2,1,0:T(4,128)(2,1)S(1)}, bf16[32,4,128]{2,1,0:T(4,128)(2,1)S(1)}, u32[]{:S(2)}, u32[]{:S(2)}) collective-permute-start(bf16[32,4,128]{2,1,0:T(4,128)(2,1)S(1)} %get-tuple-element.128), channel_id=1, source_target_pairs={{4,0},{8,4},{12,8},{16,12},{20,16},{24,20},{28,24},{5,1},{9,5},{13... | collective-permute-start | bytes 98312 | tf_op jit(solution)/shard_map/ppermute | solution.py:26
  93.0 6.4 %collective-permute-start.6 = (bf16[32,4,128]{2,1,0:T(4,128)(2,1)S(1)}, bf16[32,4,128]{2,1,0:T(4,128)(2,1)S(1)}, u32[]{:S(2)}, u32[]{:S(2)}) collective-permute-start(bf16[32,4,128]{2,1,0:T(4,128)(2,1)S(1)} %get-tuple-element.127), channel_id=1, source_target_pairs={{0,4},{4,8},{8,12},{12,16},{16,20},{20,24},{24,28},{1,5},{5,9},{9,... | collective-permute-start | bytes 98312 | tf_op jit(solution)/shard_map/ppermute | solution.py:25
  109.1 6.4 %collective-permute-start.8 = (bf16[32,4,128]{2,1,0:T(4,128)(2,1)S(1)}, bf16[32,4,128]{2,1,0:T(4,128)(2,1)S(1)}, u32[]{:S(2)}, u32[]{:S(2)}) collective-permute-start(bf16[32,4,128]{2,1,0:T(4,128)(2,1)S(1)} %get-tuple-element.120), channel_id=1, source_target_pairs={{0,4},{4,8},{8,12},{12,16},{16,20},{20,24},{24,28},{1,5},{5,9},{9,... | collective-permute-start | bytes 98312 | tf_op jit(solution)/shard_map/ppermute | solution.py:15
  113.9 7.0 %collective-permute-start.9 = (bf16[32,4,128]{2,1,0:T(4,128)(2,1)S(1)}, bf16[32,4,128]{2,1,0:T(4,128)(2,1)S(1)}, u32[]{:S(2)}, u32[]{:S(2)}) collective-permute-start(bf16[32,4,128]{2,1,0:T(4,128)(2,1)S(1)} %get-tuple-element.119), channel_id=1, source_target_pairs={{4,0},{8,4},{12,8},{16,12},{20,16},{24,20},{28,24},{5,1},{9,5},{13... | collective-permute-start | bytes 98312 | tf_op jit(solution)/shard_map/ppermute | solution.py:15
  166.9 6.1 %collective-permute-start.11 = (bf16[32,4,128]{2,1,0:T(4,128)(2,1)S(1)}, bf16[32,4,128]{2,1,0:T(4,128)(2,1)S(1)}, u32[]{:S(2)}, u32[]{:S(2)}) collective-permute-start(bf16[32,4,128]{2,1,0:T(4,128)(2,1)S(1)} %get-tuple-element.126), channel_id=1, source_target_pairs={{4,0},{8,4},{12,8},{16,12},{20,16},{24,20},{28,24},{5,1},{9,5},{13... | collective-permute-start | bytes 98312 | tf_op jit(solution)/shard_map/ppermute | solution.py:26
  168.2 6.4 %collective-permute-start.10 = (bf16[32,4,128]{2,1,0:T(4,128)(2,1)S(1)}, bf16[32,4,128]{2,1,0:T(4,128)(2,1)S(1)}, u32[]{:S(2)}, u32[]{:S(2)}) collective-permute-start(bf16[32,4,128]{2,1,0:T(4,128)(2,1)S(1)} %get-tuple-element.125), channel_id=1, source_target_pairs={{0,4},{4,8},{8,12},{12,16},{16,20},{20,24},{24,28},{1,5},{5,9},{9,... | collective-permute-start | bytes 98312 | tf_op jit(solution)/shard_map/ppermute | solution.py:25
  181.7 13.3 %copy-start.2 = (f32[32,16,128]{2,1,0:T(8,128)S(1)}, f32[32,16,128]{2,1,0:T(8,128)}, u32[]{:S(2)}) copy-start(f32[32,16,128]{2,1,0:T(8,128)} %get-tuple-element.111) | copy-start | bytes 786436
  182.3 59.2 %copy-start.1 = (f32[32,16,128]{2,1,0:T(8,128)S(1)}, f32[32,16,128]{2,1,0:T(8,128)}, u32[]{:S(2)}) copy-start(f32[32,16,128]{2,1,0:T(8,128)} %copy-done) | copy-start | bytes 786436
  182.3 59.2 %copy-start.3 = (f32[32,16,128]{2,1,0:T(8,128)S(1)}, f32[32,16,128]{2,1,0:T(8,128)}, u32[]{:S(2)}) copy-start(f32[32,16,128]{2,1,0:T(8,128)} %get-tuple-element.112) | copy-start | bytes 786436
  183.1 6.4 %collective-permute-start.12 = (bf16[32,4,128]{2,1,0:T(4,128)(2,1)S(1)}, bf16[32,4,128]{2,1,0:T(4,128)(2,1)S(1)}, u32[]{:S(2)}, u32[]{:S(2)}) collective-permute-start(bf16[32,4,128]{2,1,0:T(4,128)(2,1)S(1)} %get-tuple-element.118), channel_id=1, source_target_pairs={{0,4},{4,8},{8,12},{12,16},{16,20},{20,24},{24,28},{1,5},{5,9},{9,... | collective-permute-start | bytes 98312 | tf_op jit(solution)/shard_map/ppermute | solution.py:15
  187.9 7.0 %collective-permute-start.13 = (bf16[32,4,128]{2,1,0:T(4,128)(2,1)S(1)}, bf16[32,4,128]{2,1,0:T(4,128)(2,1)S(1)}, u32[]{:S(2)}, u32[]{:S(2)}) collective-permute-start(bf16[32,4,128]{2,1,0:T(4,128)(2,1)S(1)} %get-tuple-element.117), channel_id=1, source_target_pairs={{4,0},{8,4},{12,8},{16,12},{20,16},{24,20},{28,24},{5,1},{9,5},{13... | collective-permute-start | bytes 98312 | tf_op jit(solution)/shard_map/ppermute | solution.py:15
where the time goes:
time: 244 us; the launch traced here: 243 us
  blocking collectives  124 us (51%)
  starting transfers between devices  43.2 us (18%)
  matrix products  29.9 us (12%)
  waiting for transfers between devices  26 us (11%)
  between operations  11.3 us (5%)
  other arithmetic  7.49 us (3%)
    psum x3, blocking collectives, paired(): lax.psum((local_inner(vector, vector), local_inner(vector, applied)), ('t...  124 us
    ppermute x8, starting transfers between devices, from_behind(): return lax.ppermute(value, axis, pairs)  24.5 us
    dot_general x4, matrix products, adjoint_image(): jnp.einsum('cwgf,cgrsf->cwgrs', image16, kernels, preferred_element_type=...  22 us
    ppermute x8, waiting for transfers between devices, from_behind(): return lax.ppermute(value, axis, pairs)  21.5 us
    ppermute x3, starting transfers between devices, extended(): before = lax.ppermute(last, axis, up)  14.8 us
  transfers between devices with their start and end apart: 14, of which 11 were waited for; matrix products, arithmetic and copies ran while one was open for 0% of the time, Pallas kernels for 0%

commit v1 on v0

--- a/solution.py
+++ b/solution.py
@@ -2,11 +2,13 @@
 import jax.numpy as jnp
 from jax import lax
 from jax.sharding import PartitionSpec as P
+from jax.lax import psum
 
 HALO_BLOCKS = 4
 BLOCKS_DEV = 16
 ITERATIONS = 3
 TIKHONOV = 0.5
+map_the_hubs = lambda field_in: psum(psum(field_in, axis_name="wave"), axis_name="tile")
 
 
 def from_behind(value, axis, by):
@@ -95,9 +97,7 @@
     residual = rhs
 
     def paired(vector, applied):
-        return lax.psum(
-            (local_inner(vector, vector), local_inner(vector, applied)), ("tile", "wave")
-        )
+        return map_the_hubs((local_inner(vector, vector), local_inner(vector, applied)))
 
     applied = operate(residual)
     current, product = paired(residual, applied)

time: 244 us -> 196 us (0.80)
  blocking collectives: 124 us -> 80.1 us
    psum x3 -> x6, blocking collectives: 124 us -> 80.1 us  [the longest x3 61.2 us: psum(psum(field_in, axis_name='wave'), axis_name='tile')]
where the time goes in v1:
time: 196 us; the launch traced here: 195 us
  blocking collectives  80.1 us (41%)
  starting transfers between devices  41.4 us (21%)
  matrix products  29.9 us (15%)
  waiting for transfers between devices  23.6 us (12%)
  between operations  12 us (6%)
  other arithmetic  7.54 us (4%)
    psum x3, blocking collectives, psum(psum(field_in, axis_name='wave'), axis_name='tile')  61.2 us
    ppermute x8, starting transfers between devices, from_behind(): return lax.ppermute(value, axis, pairs)  23.3 us
    dot_general x4, matrix products, adjoint_image(): jnp.einsum('cwgf,cgrsf->cwgrs', image16, kernels, preferred_element_type=...  22 us
    ppermute x8, waiting for transfers between devices, from_behind(): return lax.ppermute(value, axis, pairs)  19.1 us
    psum x3, blocking collectives, psum(field_in, axis_name='wave')  18.9 us
    ppermute x3, starting transfers between devices, extended(): before = lax.ppermute(last, axis, up)  14.3 us
    ppermute x3, waiting for transfers between devices, extended(): before = lax.ppermute(last, axis, up)  4.51 us
  transfers between devices with their start and end apart: 14, of which 11 were waited for; matrix products, arithmetic and copies ran while one was open for 0% of the time, Pallas kernels for 0%

profile of v1, /device:TPU:0, one launch (start us, length us, event | category | flops | bytes accessed | tf_op | source)
XLA Modules:
  0.0 195.2 jit_solution(14319018164506953052)
XLA Ops:
  1.3 1.0 multiply_bitcast_fusion
  2.3 3.7 %fusion.12 = f32[32,32,4,128]{3,1,2,0:T(8,128)S(1)} fusion(bf16[1,32,4,128,128]{4,3,2,1,0:T(8,128)(2,1)} %param.21, bf16[32,32,128,1]{2,1,0,3:T(8,128)(2,1)S(1)} %multiply_bitcast_fusion), kind=kOutput, calls=%fused_computation.12 | convolution fusion | flops 134217728 | bytes 6553600 | tf_op jit(solution)/shard_map/cwgf,cgrsf->cwgrs/dot_general | solution.py:50
  6.1 0.3 fusion.71
  6.4 0.0 copy-start.4
  6.4 0.3 fusion.89
  6.6 0.4 copy-done.4
  7.0 0.7 convolution_bitcast_fusion.6
  7.7 0.7 fusion.153
  8.4 4.9 %collective-permute-start = (bf16[32,4,128]{2,1,0:T(4,128)(2,1)S(1)}, bf16[32,4,128]{2,1,0:T(4,128)(2,1)S(1)}, u32[]{:S(2)}, u32[]{:S(2)}) collective-permute-start(bf16[32,4,128]{2,1,0:T(4,128)(2,1)S(1)} %get-tuple-element.130), channel_id=1, source_target_pairs={{0,4},{4,8},{8,12},{12,16},{16,20},{20,24},{24,28},{1,5},{5,9},{9,... | collective-permute-start | bytes 98312 | tf_op jit(solution)/shard_map/ppermute | solution.py:17
  13.3 1.3 collective-permute-start.1
  14.7 0.2 collective-permute-done
  14.9 4.2 %collective-permute-done.1 = bf16[32,4,128]{2,1,0:T(4,128)(2,1)S(1)} collective-permute-done((bf16[32,4,128]{2,1,0:T(4,128)(2,1)S(1)}, bf16[32,4,128]{2,1,0:T(4,128)(2,1)S(1)}, u32[]{:S(2)}, u32[]{:S(2)}) %collective-permute-start.1) | collective-permute-done | bytes 32800 | tf_op jit(solution)/shard_map/ppermute | solution.py:17
  19.2 1.3 collective-permute-start.3
  20.5 5.0 %collective-permute-start.2 = (bf16[32,4,128]{2,1,0:T(4,128)(2,1)S(1)}, bf16[32,4,128]{2,1,0:T(4,128)(2,1)S(1)}, u32[]{:S(2)}, u32[]{:S(2)}) collective-permute-start(bf16[32,4,128]{2,1,0:T(4,128)(2,1)S(1)} %get-tuple-element.135), channel_id=1, source_target_pairs={{0,4},{4,8},{8,12},{12,16},{16,20},{20,24},{24,28},{1,5},{5,9},{9,... | collective-permute-start | bytes 98312 | tf_op jit(solution)/shard_map/ppermute | solution.py:27
  25.5 0.0 collective-permute-done.3
  25.6 1.6 collective-permute-done.2
  27.1 0.5 fusion.18
  27.6 6.0 %fusion.8 = f32[32,32,4,128]{3,1,2,0:T(8,128)S(1)} fusion(bf16[1,32,4,128,128]{4,3,2,1,0:T(8,128)(2,1)} %param.21, bf16[32,32,4,128]{3,1,2,0:T(8,128)(2,1)S(1)} %fusion.18, f32[32]{0:T(128)S(1)} %compare_convert_fusion), kind=kOutput, calls=%fused_computation.8 | convolution fusion | flops 268697600 | bytes 7340160 | tf_op jit(solution)/shard_map/cwgf,cgrsf->cwgrs/dot_general | solution.py:50
  33.6 0.3 fusion.72
  33.9 0.2 fusion.90
  34.2 0.7 convolution_bitcast_fusion.4
  34.8 0.7 fusion.154
  35.6 4.8 %collective-permute-start.4 = (bf16[32,4,128]{2,1,0:T(4,128)(2,1)S(1)}, bf16[32,4,128]{2,1,0:T(4,128)(2,1)S(1)}, u32[]{:S(2)}, u32[]{:S(2)}) collective-permute-start(bf16[32,4,128]{2,1,0:T(4,128)(2,1)S(1)} %get-tuple-element.128), channel_id=1, source_target_pairs={{0,4},{4,8},{8,12},{12,16},{16,20},{20,24},{24,28},{1,5},{5,9},{9,... | collective-permute-start | bytes 98312 | tf_op jit(solution)/shard_map/ppermute | solution.py:17
  40.4 1.3 collective-permute-start.5
  41.7 0.2 collective-permute-done.4
  42.0 5.4 %collective-permute-done.5 = bf16[32,4,128]{2,1,0:T(4,128)(2,1)S(1)} collective-permute-done((bf16[32,4,128]{2,1,0:T(4,128)(2,1)S(1)}, bf16[32,4,128]{2,1,0:T(4,128)(2,1)S(1)}, u32[]{:S(2)}, u32[]{:S(2)}) %collective-permute-start.5) | collective-permute-done | bytes 32800 | tf_op jit(solution)/shard_map/ppermute | solution.py:17
  47.5 0.7 multiply_reduce_fusion.4
  48.2 6.3 %all-reduce.5 = (f32[]{:T(128)}, f32[]{:T(128)}) all-reduce(f32[]{:T(128)} %get-tuple-element.103, f32[]{:T(128)} %get-tuple-element.102), channel_id=1, replica_groups=mesh['tile'=8,'wave'=4] {'wave'}, use_global_device_ids=true, to_apply=%region_1.0 | all-reduce | flops 2 | bytes 16 | tf_op jit(solution)/shard_map/psum | solution.py:11
  54.4 20.9 %all-reduce.2 = (f32[]{:T(128)}, f32[]{:T(128)}) all-reduce(f32[]{:T(128)} %get-tuple-element.114, f32[]{:T(128)} %get-tuple-element.115), channel_id=1, replica_groups=mesh['tile'=8,'wave'=4] {'tile'}, use_global_device_ids=true, to_apply=%region_2.0 | all-reduce | flops 2 | bytes 16 | tf_op jit(solution)/shard_map/psum | solution.py:11
  76.8 1.3 collective-permute-start.7
  78.1 4.7 %collective-permute-start.6 = (bf16[32,4,128]{2,1,0:T(4,128)(2,1)S(1)}, bf16[32,4,128]{2,1,0:T(4,128)(2,1)S(1)}, u32[]{:S(2)}, u32[]{:S(2)}) collective-permute-start(bf16[32,4,128]{2,1,0:T(4,128)(2,1)S(1)} %get-tuple-element.133), channel_id=1, source_target_pairs={{0,4},{4,8},{8,12},{12,16},{16,20},{20,24},{24,28},{1,5},{5,9},{9,... | collective-permute-start | bytes 98312 | tf_op jit(solution)/shard_map/ppermute | solution.py:27
  82.8 1.4 collective-permute-done.6
  84.2 1.5 fusion.19
  85.6 6.3 %fusion.4 = f32[32,32,4,128]{3,1,2,0:T(8,128)S(1)} fusion(bf16[1,32,4,128,128]{4,3,2,1,0:T(8,128)(2,1)} %param.21, bf16[32,32,4,128]{3,1,2,0:T(8,128)(2,1)} %fusion.19, f32[32]{0:T(128)S(1)} %compare_convert_fusion), kind=kOutput, calls=%fused_computation.4 | convolution fusion | flops 268697600 | bytes 7340160 | tf_op jit(solution)/shard_map/cwgf,cgrsf->cwgrs/dot_general | solution.py:50
  92.0 0.3 fusion.73
  92.2 0.2 fusion.91
  92.5 0.7 convolution_bitcast_fusion.2
  93.2 0.7 fusion.155
  93.9 4.2 %collective-permute-start.8 = (bf16[32,4,128]{2,1,0:T(4,128)(2,1)S(1)}, bf16[32,4,128]{2,1,0:T(4,128)(2,1)S(1)}, u32[]{:S(2)}, u32[]{:S(2)}) collective-permute-start(bf16[32,4,128]{2,1,0:T(4,128)(2,1)S(1)} %get-tuple-element.126), channel_id=1, source_target_pairs={{0,4},{4,8},{8,12},{12,16},{16,20},{20,24},{24,28},{1,5},{5,9},{9,... | collective-permute-start | bytes 98312 | tf_op jit(solution)/shard_map/ppermute | solution.py:17
  98.1 1.3 collective-permute-start.9
  99.4 0.2 collective-permute-done.8
  99.7 4.2 %collective-permute-done.9 = bf16[32,4,128]{2,1,0:T(4,128)(2,1)S(1)} collective-permute-done((bf16[32,4,128]{2,1,0:T(4,128)(2,1)S(1)}, bf16[32,4,128]{2,1,0:T(4,128)(2,1)S(1)}, u32[]{:S(2)}, u32[]{:S(2)}) %collective-permute-start.9) | collective-permute-done | bytes 32800 | tf_op jit(solution)/shard_map/ppermute | solution.py:17
  104.0 0.7 multiply_reduce_fusion.2
  104.7 6.3 %all-reduce.4 = (f32[]{:T(128)}, f32[]{:T(128)}) all-reduce(f32[]{:T(128)} %get-tuple-element.101, f32[]{:T(128)} %get-tuple-element.100), channel_id=1, replica_groups=mesh['tile'=8,'wave'=4] {'wave'}, use_global_device_ids=true, to_apply=%region_7.0 | all-reduce | flops 2 | bytes 16 | tf_op jit(solution)/shard_map/psum | solution.py:11
  111.1 19.6 %all-reduce.1 = (f32[]{:T(128)}, f32[]{:T(128)}) all-reduce(f32[]{:T(128)} %get-tuple-element.112, f32[]{:T(128)} %get-tuple-element.113), channel_id=1, replica_groups=mesh['tile'=8,'wave'=4] {'tile'}, use_global_device_ids=true, to_apply=%region_8.0 | all-reduce | flops 2 | bytes 16 | tf_op jit(solution)/shard_map/psum | solution.py:11
  135.4 0.9 fusion.144
  136.3 1.3 collective-permute-start.11
  137.7 4.5 %collective-permute-start.10 = (bf16[32,4,128]{2,1,0:T(4,128)(2,1)S(1)}, bf16[32,4,128]{2,1,0:T(4,128)(2,1)S(1)}, u32[]{:S(2)}, u32[]{:S(2)}) collective-permute-start(bf16[32,4,128]{2,1,0:T(4,128)(2,1)S(1)} %get-tuple-element.131), channel_id=1, source_target_pairs={{0,4},{4,8},{8,12},{12,16},{16,20},{20,24},{24,28},{1,5},{5,9},{9,... | collective-permute-start | bytes 98312 | tf_op jit(solution)/shard_map/ppermute | solution.py:27
  142.2 1.6 collective-permute-done.10
  143.8 0.5 fusion.20
  144.3 6.0 %fusion = f32[32,32,4,128]{3,1,2,0:T(8,128)S(1)} fusion(bf16[1,32,4,128,128]{4,3,2,1,0:T(8,128)(2,1)} %param.21, bf16[32,32,4,128]{3,1,2,0:T(8,128)(2,1)S(1)} %fusion.20, f32[32]{0:T(128)S(1)} %compare_convert_fusion), kind=kOutput, calls=%fused_computation | convolution fusion | flops 268697600 | bytes 7340160 | tf_op jit(solution)/shard_map/cwgf,cgrsf->cwgrs/dot_general | solution.py:50
  150.3 0.3 fusion.74
  150.6 0.2 fusion.92
  150.8 0.0 copy-start.2
  150.8 0.7 convolution_bitcast_fusion
  151.5 0.7 fusion.156
  152.3 4.2 %collective-permute-start.12 = (bf16[32,4,128]{2,1,0:T(4,128)(2,1)S(1)}, bf16[32,4,128]{2,1,0:T(4,128)(2,1)S(1)}, u32[]{:S(2)}, u32[]{:S(2)}) collective-permute-start(bf16[32,4,128]{2,1,0:T(4,128)(2,1)S(1)} %get-tuple-element.124), channel_id=1, source_target_pairs={{0,4},{4,8},{8,12},{12,16},{16,20},{20,24},{24,28},{1,5},{5,9},{9,... | collective-permute-start | bytes 98312 | tf_op jit(solution)/shard_map/ppermute | solution.py:17
  156.5 1.3 collective-permute-start.13
  157.8 0.2 collective-permute-done.12
  158.1 4.2 %collective-permute-done.13 = bf16[32,4,128]{2,1,0:T(4,128)(2,1)S(1)} collective-permute-done((bf16[32,4,128]{2,1,0:T(4,128)(2,1)S(1)}, bf16[32,4,128]{2,1,0:T(4,128)(2,1)S(1)}, u32[]{:S(2)}, u32[]{:S(2)}) %collective-permute-start.13) | collective-permute-done | bytes 32800 | tf_op jit(solution)/shard_map/ppermute | solution.py:17
  162.4 0.8 multiply_reduce_fusion
  163.1 6.3 %all-reduce.3 = (f32[]{:T(128)}, f32[]{:T(128)}) all-reduce(f32[]{:T(128)} %get-tuple-element.99, f32[]{:T(128)} %get-tuple-element.98), channel_id=1, replica_groups=mesh['tile'=8,'wave'=4] {'wave'}, use_global_device_ids=true, to_apply=%region_13.0 | all-reduce | flops 2 | bytes 16 | tf_op jit(solution)/shard_map/psum | solution.py:11
  169.4 20.7 %all-reduce = (f32[]{:T(128)}, f32[]{:T(128)}) all-reduce(f32[]{:T(128)} %get-tuple-element.110, f32[]{:T(128)} %get-tuple-element.111), channel_id=1, replica_groups=mesh['tile'=8,'wave'=4] {'tile'}, use_global_device_ids=true, to_apply=%region_14.0 | all-reduce | flops 2 | bytes 16 | tf_op jit(solution)/shard_map/psum | solution.py:11
  194.3 0.9 multiply_subtract_fusion
  (33 shorter events, 0.7 us)
Async XLA Ops:
  6.4 0.7 copy-start.4
  8.4 6.5 %collective-permute-start = (bf16[32,4,128]{2,1,0:T(4,128)(2,1)S(1)}, bf16[32,4,128]{2,1,0:T(4,128)(2,1)S(1)}, u32[]{:S(2)}, u32[]{:S(2)}) collective-permute-start(bf16[32,4,128]{2,1,0:T(4,128)(2,1)S(1)} %get-tuple-element.130), channel_id=1, source_target_pairs={{0,4},{4,8},{8,12},{12,16},{16,20},{20,24},{24,28},{1,5},{5,9},{9,... | collective-permute-start | bytes 98312 | tf_op jit(solution)/shard_map/ppermute | solution.py:17
  13.3 5.8 %collective-permute-start.1 = (bf16[32,4,128]{2,1,0:T(4,128)(2,1)S(1)}, bf16[32,4,128]{2,1,0:T(4,128)(2,1)S(1)}, u32[]{:S(2)}, u32[]{:S(2)}) collective-permute-start(bf16[32,4,128]{2,1,0:T(4,128)(2,1)S(1)} %get-tuple-element.129), channel_id=1, source_target_pairs={{4,0},{8,4},{12,8},{16,12},{20,16},{24,20},{28,24},{5,1},{9,5},{13... | collective-permute-start | bytes 98312 | tf_op jit(solution)/shard_map/ppermute | solution.py:17
  19.2 6.3 %collective-permute-start.3 = (bf16[32,4,128]{2,1,0:T(4,128)(2,1)S(1)}, bf16[32,4,128]{2,1,0:T(4,128)(2,1)S(1)}, u32[]{:S(2)}, u32[]{:S(2)}) collective-permute-start(bf16[32,4,128]{2,1,0:T(4,128)(2,1)S(1)} %get-tuple-element.136), channel_id=1, source_target_pairs={{4,0},{8,4},{12,8},{16,12},{20,16},{24,20},{28,24},{5,1},{9,5},{13... | collective-permute-start | bytes 98312 | tf_op jit(solution)/shard_map/ppermute | solution.py:28
  20.5 6.6 %collective-permute-start.2 = (bf16[32,4,128]{2,1,0:T(4,128)(2,1)S(1)}, bf16[32,4,128]{2,1,0:T(4,128)(2,1)S(1)}, u32[]{:S(2)}, u32[]{:S(2)}) collective-permute-start(bf16[32,4,128]{2,1,0:T(4,128)(2,1)S(1)} %get-tuple-element.135), channel_id=1, source_target_pairs={{0,4},{4,8},{8,12},{12,16},{16,20},{20,24},{24,28},{1,5},{5,9},{9,... | collective-permute-start | bytes 98312 | tf_op jit(solution)/shard_map/ppermute | solution.py:27
  35.6 6.4 %collective-permute-start.4 = (bf16[32,4,128]{2,1,0:T(4,128)(2,1)S(1)}, bf16[32,4,128]{2,1,0:T(4,128)(2,1)S(1)}, u32[]{:S(2)}, u32[]{:S(2)}) collective-permute-start(bf16[32,4,128]{2,1,0:T(4,128)(2,1)S(1)} %get-tuple-element.128), channel_id=1, source_target_pairs={{0,4},{4,8},{8,12},{12,16},{16,20},{20,24},{24,28},{1,5},{5,9},{9,... | collective-permute-start | bytes 98312 | tf_op jit(solution)/shard_map/ppermute | solution.py:17
  40.4 7.0 %collective-permute-start.5 = (bf16[32,4,128]{2,1,0:T(4,128)(2,1)S(1)}, bf16[32,4,128]{2,1,0:T(4,128)(2,1)S(1)}, u32[]{:S(2)}, u32[]{:S(2)}) collective-permute-start(bf16[32,4,128]{2,1,0:T(4,128)(2,1)S(1)} %get-tuple-element.127), channel_id=1, source_target_pairs={{4,0},{8,4},{12,8},{16,12},{20,16},{24,20},{28,24},{5,1},{9,5},{13... | collective-permute-start | bytes 98312 | tf_op jit(solution)/shard_map/ppermute | solution.py:17
  76.7 58.7 %copy-start = (f32[32,16,128]{2,1,0:T(8,128)}, f32[32,16,128]{2,1,0:T(8,128)S(1)}, u32[]{:S(2)}) copy-start(f32[32,16,128]{2,1,0:T(8,128)S(1)} %get-tuple-element.120) | copy-start | bytes 786436
  76.8 6.0 %collective-permute-start.7 = (bf16[32,4,128]{2,1,0:T(4,128)(2,1)S(1)}, bf16[32,4,128]{2,1,0:T(4,128)(2,1)S(1)}, u32[]{:S(2)}, u32[]{:S(2)}) collective-permute-start(bf16[32,4,128]{2,1,0:T(4,128)(2,1)S(1)} %get-tuple-element.134), channel_id=1, source_target_pairs={{4,0},{8,4},{12,8},{16,12},{20,16},{24,20},{28,24},{5,1},{9,5},{13... | collective-permute-start | bytes 98312 | tf_op jit(solution)/shard_map/ppermute | solution.py:28
  78.1 6.1 %collective-permute-start.6 = (bf16[32,4,128]{2,1,0:T(4,128)(2,1)S(1)}, bf16[32,4,128]{2,1,0:T(4,128)(2,1)S(1)}, u32[]{:S(2)}, u32[]{:S(2)}) collective-permute-start(bf16[32,4,128]{2,1,0:T(4,128)(2,1)S(1)} %get-tuple-element.133), channel_id=1, source_target_pairs={{0,4},{4,8},{8,12},{12,16},{16,20},{20,24},{24,28},{1,5},{5,9},{9,... | collective-permute-start | bytes 98312 | tf_op jit(solution)/shard_map/ppermute | solution.py:27
  93.9 5.8 %collective-permute-start.8 = (bf16[32,4,128]{2,1,0:T(4,128)(2,1)S(1)}, bf16[32,4,128]{2,1,0:T(4,128)(2,1)S(1)}, u32[]{:S(2)}, u32[]{:S(2)}) collective-permute-start(bf16[32,4,128]{2,1,0:T(4,128)(2,1)S(1)} %get-tuple-element.126), channel_id=1, source_target_pairs={{0,4},{4,8},{8,12},{12,16},{16,20},{20,24},{24,28},{1,5},{5,9},{9,... | collective-permute-start | bytes 98312 | tf_op jit(solution)/shard_map/ppermute | solution.py:17
  98.1 5.8 %collective-permute-start.9 = (bf16[32,4,128]{2,1,0:T(4,128)(2,1)S(1)}, bf16[32,4,128]{2,1,0:T(4,128)(2,1)S(1)}, u32[]{:S(2)}, u32[]{:S(2)}) collective-permute-start(bf16[32,4,128]{2,1,0:T(4,128)(2,1)S(1)} %get-tuple-element.125), channel_id=1, source_target_pairs={{4,0},{8,4},{12,8},{16,12},{20,16},{24,20},{28,24},{5,1},{9,5},{13... | collective-permute-start | bytes 98312 | tf_op jit(solution)/shard_map/ppermute | solution.py:17
  136.3 5.9 %collective-permute-start.11 = (bf16[32,4,128]{2,1,0:T(4,128)(2,1)S(1)}, bf16[32,4,128]{2,1,0:T(4,128)(2,1)S(1)}, u32[]{:S(2)}, u32[]{:S(2)}) collective-permute-start(bf16[32,4,128]{2,1,0:T(4,128)(2,1)S(1)} %get-tuple-element.132), channel_id=1, source_target_pairs={{4,0},{8,4},{12,8},{16,12},{20,16},{24,20},{28,24},{5,1},{9,5},{13... | collective-permute-start | bytes 98312 | tf_op jit(solution)/shard_map/ppermute | solution.py:28
  137.7 6.1 %collective-permute-start.10 = (bf16[32,4,128]{2,1,0:T(4,128)(2,1)S(1)}, bf16[32,4,128]{2,1,0:T(4,128)(2,1)S(1)}, u32[]{:S(2)}, u32[]{:S(2)}) collective-permute-start(bf16[32,4,128]{2,1,0:T(4,128)(2,1)S(1)} %get-tuple-element.131), channel_id=1, source_target_pairs={{0,4},{4,8},{8,12},{12,16},{16,20},{20,24},{24,28},{1,5},{5,9},{9,... | collective-permute-start | bytes 98312 | tf_op jit(solution)/shard_map/ppermute | solution.py:27
  150.8 11.5 %copy-start.2 = (f32[32,16,128]{2,1,0:T(8,128)S(1)}, f32[32,16,128]{2,1,0:T(8,128)}, u32[]{:S(2)}) copy-start(f32[32,16,128]{2,1,0:T(8,128)} %get-tuple-element.117) | copy-start | bytes 786436
  151.5 42.8 %copy-start.1 = (f32[32,16,128]{2,1,0:T(8,128)S(1)}, f32[32,16,128]{2,1,0:T(8,128)}, u32[]{:S(2)}) copy-start(f32[32,16,128]{2,1,0:T(8,128)} %copy-done) | copy-start | bytes 786436
  151.5 42.8 %copy-start.3 = (f32[32,16,128]{2,1,0:T(8,128)S(1)}, f32[32,16,128]{2,1,0:T(8,128)}, u32[]{:S(2)}) copy-start(f32[32,16,128]{2,1,0:T(8,128)} %get-tuple-element.118) | copy-start | bytes 786436
  152.3 5.8 %collective-permute-start.12 = (bf16[32,4,128]{2,1,0:T(4,128)(2,1)S(1)}, bf16[32,4,128]{2,1,0:T(4,128)(2,1)S(1)}, u32[]{:S(2)}, u32[]{:S(2)}) collective-permute-start(bf16[32,4,128]{2,1,0:T(4,128)(2,1)S(1)} %get-tuple-element.124), channel_id=1, source_target_pairs={{0,4},{4,8},{8,12},{12,16},{16,20},{20,24},{24,28},{1,5},{5,9},{9,... | collective-permute-start | bytes 98312 | tf_op jit(solution)/shard_map/ppermute | solution.py:17
  156.5 5.8 %collective-permute-start.13 = (bf16[32,4,128]{2,1,0:T(4,128)(2,1)S(1)}, bf16[32,4,128]{2,1,0:T(4,128)(2,1)S(1)}, u32[]{:S(2)}, u32[]{:S(2)}) collective-permute-start(bf16[32,4,128]{2,1,0:T(4,128)(2,1)S(1)} %get-tuple-element.123), channel_id=1, source_target_pairs={{4,0},{8,4},{12,8},{16,12},{20,16},{24,20},{28,24},{5,1},{9,5},{13... | collective-permute-start | bytes 98312 | tf_op jit(solution)/shard_map/ppermute | solution.py:17
